TPU v7x, 256 devices: a whole 4x4x8 slice. The times are simulated.
256 devices in a mesh: seq: 32 (over y, z), wide: 8 (over x, core).
Axes of the slice: x: 4, y: 4, z: 8, core: 2. Of those that a mesh axis runs over, the one named last changes fastest.
Arguments:
- queries: bfloat16 [16384, 4096], P('seq', 'wide'), may hold values from -500 to 500
- keys: bfloat16 [16384, 4096], P('seq', 'wide'), may hold values from -500 to 500
- values: bfloat16 [16384, 4096], P('seq', 'wide'), may hold values from -6 to 6
- log_decay: float32 [16384, 32], P('seq', 'wide'), may hold values from -0.8 to 0, as said below
- ridge: float32 [4096], P('wide'), may hold values from 0.05 to 2
- out_weight: bfloat16 [4096, 4096], P('wide'), may hold values from -0.09375 to 0.09375
Outputs:
- mixed: bfloat16 [16384, 4096], P(('seq', 'wide'))
Inputs may be any that keep to these rules, and one draw needn't show every extreme that they name: `log_decay`: negative.
All inputs are finite; a program needn't handle non-finite values.
Results may differ from a plain program's by a relative error of at most 0.0065.
Values sent between devices are 32-bit elements; how exact they have to be, the bound alone decides.
A program may use at most 128 MiB of HBM per device.

v0:
```python
import jax
import jax.numpy as jnp
from jax import lax
from jax.sharding import PartitionSpec as P

HD = 128
SPAN = 128
ITERS = 8
highest = lax.Precision.HIGHEST


def unit_rows(matrix, head_count, head_size):
    entries = matrix.astype(jnp.float32).reshape(matrix.shape[0], head_count, head_size)
    return entries * lax.rsqrt(jnp.sum(entries * entries, axis=-1, keepdims=True) + 1e-06)


def span_read(query, key_rows, value_rows, cumulative, state_h, state_g, ridge_rows):
    length = query.shape[-2]
    places = jnp.arange(length)
    causal = places[:, None] >= places[None, :]
    spread = cumulative[..., :, None] - cumulative[..., None, :]
    weight = jnp.where(causal, jnp.exp(jnp.where(causal, spread, 0.0)), 0.0)
    opening = jnp.exp(cumulative)[..., None]
    solved = jnp.zeros_like(query)
    residual = query
    direction = query
    norm_now = jnp.sum(residual * residual, axis=-1, keepdims=True)
    for sweep in range(ITERS):
        operate_scores = (
            jnp.einsum("...td,...sd->...ts", direction, key_rows, precision=highest) * weight
        )
        operate_carried = jnp.einsum("...td,...ed->...te", direction, state_h, precision=highest)
        local_part = jnp.einsum("...ts,...sd->...td", operate_scores, key_rows, precision=highest)
        image = opening * operate_carried + local_part + ridge_rows * direction
        alpha = norm_now / jnp.sum(direction * image, axis=-1, keepdims=True)
        solved = solved + alpha * direction
        residual = residual - alpha * image
        norm_next = jnp.sum(residual * residual, axis=-1, keepdims=True)
        direction = residual + norm_next / norm_now * direction
        norm_now = norm_next
    scores = jnp.einsum("...td,...sd->...ts", solved, key_rows, precision=highest) * weight
    carried = jnp.einsum("...td,...ed->...te", solved, state_g, precision=highest)
    return opening * carried + jnp.einsum(
        "...ts,...se->...te", scores, value_rows, precision=highest
    )


def span_summary(key_rows, value_rows, cumulative):
    closing = cumulative[..., -1]
    fading = jnp.exp(closing[..., None] - cumulative)[..., None]
    gram = jnp.einsum("...sd,...se->...de", key_rows * fading, key_rows, precision=highest)
    memory = jnp.einsum("...se,...sd->...ed", value_rows * fading, key_rows, precision=highest)
    return (closing, gram, memory)


def combine_memories(earlier, later):
    factor = jnp.exp(later[2])[:, None, None]
    return (factor * earlier[0] + later[0], factor * earlier[1] + later[1], earlier[2] + later[2])


def body(queries, keys, values, log_decay, ridge, out_weight):
    rows_dev = queries.shape[0]
    head_count = log_decay.shape[1]
    head_size = HD
    block_list = rows_dev // SPAN

    def arrange(entries):
        return entries.reshape(block_list, SPAN, head_count, head_size).transpose(2, 0, 1, 3)

    query_rows = arrange(unit_rows(queries, head_count, head_size))
    key_rows = arrange(unit_rows(keys, head_count, head_size))
    value_rows = arrange(values.astype(jnp.float32).reshape(rows_dev, head_count, head_size))
    cumulative = jnp.cumsum(
        log_decay.reshape(block_list, SPAN, head_count).transpose(2, 0, 1), axis=-1
    )
    ridge_rows = ridge.reshape(head_count, 1, 1, head_size)
    closing, gram, memory = span_summary(key_rows, value_rows, cumulative)

    def running_summation(carry, items):
        return (combine_memories(carry, items), carry)

    blank_state = jnp.zeros((head_count, head_size, head_size), jnp.float32)
    blank_decay = jnp.zeros((head_count,), jnp.float32)
    shard_resident_carry, before = lax.scan(
        running_summation,
        (blank_state, blank_state, blank_decay),
        (gram.transpose(1, 0, 2, 3), memory.transpose(1, 0, 2, 3), closing.T),
    )
    device_h, device_g, device_decay = shard_resident_carry
    preceding_memory_h, incoming_gram_matrix, before_decay = before
    totals = lax.all_gather(device_decay[None], "seq", axis=0, tiled=True)
    position = lax.axis_index("seq")
    inclusive = jnp.cumsum(totals, axis=0)
    exclusive = inclusive - totals
    mine = lax.dynamic_index_in_dim(exclusive, position, 0, keepdims=False)
    preceding_rows = (jnp.arange(totals.shape[0]) < position)[:, None]
    lags = mine[None, :] - inclusive
    weights = jnp.where(preceding_rows, jnp.exp(jnp.where(preceding_rows, lags, 0.0)), 0.0)
    added_h = jnp.einsum(
        "jh,jhde->hde",
        weights,
        lax.all_gather(device_h[None], "seq", axis=0, tiled=True),
        precision=highest,
    )
    added_g = jnp.einsum(
        "jh,jhde->hde",
        weights,
        lax.all_gather(device_g[None], "seq", axis=0, tiled=True),
        precision=highest,
    )
    lifted = jnp.exp(before_decay)[..., None, None]
    start_h = (lifted * added_h[None] + preceding_memory_h).transpose(1, 0, 2, 3)
    start_g = (lifted * added_g[None] + incoming_gram_matrix).transpose(1, 0, 2, 3)
    reads = span_read(query_rows, key_rows, value_rows, cumulative, start_h, start_g, ridge_rows)
    reads = reads.transpose(1, 2, 0, 3).reshape(rows_dev, head_count, head_size)
    normed = reads * lax.rsqrt(jnp.mean(reads * reads, axis=-1, keepdims=True) + 1e-06)
    normed = normed.reshape(rows_dev, head_count * head_size).astype(jnp.bfloat16)
    mixed = lax.psum_scatter(
        jnp.dot(normed, out_weight, preferred_element_type=jnp.float32),
        "wide",
        scatter_dimension=0,
        tiled=True,
    )
    return mixed.astype(jnp.bfloat16)


def solution(mesh):
    placed = (
        P("seq", "wide"),
        P("seq", "wide"),
        P("seq", "wide"),
        P("seq", "wide"),
        P("wide"),
        P("wide", None),
    )
    return jax.shard_map(
        body, mesh=mesh, in_specs=placed, out_specs=P(("seq", "wide"), None), check_vma=False
    )
```

profile of v0, /device:TPU:1, one launch (start us, length us, event | category | flops | bytes accessed | tf_op | source)
XLA Modules:
  0.0 367.5 jit_solution(1191460066784433861)
XLA Ops:
  12.7 1.9 reduce_sum.173
  15.6 2.3 fusion.10
  17.9 3.2 convolution_bitcast_fusion.1
  23.5 8.0 %while.21 = (s32[]{:T(128)}, f32[4,128,128]{2,1,0:T(8,128)S(1)}, f32[4,128,128]{2,1,0:T(8,128)S(1)}, f32[4]{0:T(128)S(1)}, f32[4,4,128,128]{3,2,1,0:T(8,128)}, /...) while((s32[]{:T(128)}, f32[4,128,128]{2,1,0:T(8,128)S(1)}, ...), condition=%wide.region_5.6_spmd.clone, body=%wide.region_4.5_spmd.clone.sunk | while | flops 524299 | bytes 2622221 | solution.py:84
  34.4 65.5 %all-reduce = f32[128]{0:T(128)S(1)} all-reduce(f32[128]{0:T(128)S(1)} %dynamic-update-slice), channel_id=2, replica_groups=mesh['seq'=32,'wide'=8] {'seq'}, use_global_device_ids=true, to_apply=%add | all-reduce | flops 128 | bytes 1024
  100.2 2.4 reshape.176
  102.6 2.2 convert_multiply_fusion.1
  107.1 1.6 copy.60
  108.8 3.0 convolution_multiply_fusion.15
  111.8 21.4 %all-gather.6.cloned.1.call-done = f32[128,128,128]{2,1,0:T(8,128)} async-done(((f32[4,128,128]{2,1,0:T(8,128)}), f32[128,128,128]{2,1,0:T(8,128)}) %all-gather.6.cloned.1.call-update) | async-done | bytes 8388624 | tf_op jit(solution)/shard_map/all_gather | solution.py:102
  133.3 12.0 %fusion.6 = f32[4,1,128,128]{3,1,2,0:T(1,128)S(1)} fusion(f32[32,4,1,1]{0,2,3,1:T(1,128)S(1)} %copy.109, f32[32,4,128,128]{3,2,1,0:T(8,128)} %bitcast.204), kind=kOutput, calls=%fused_computation.12 | convolution fusion | flops 25165824 | bytes 8651264 | tf_op jit(solution)/shard_map/jh,jhde->hde/dot_general | solution.py:99
  145.3 85.5 %all-gather.8.cloned.1.call-done = f32[128,128,128]{2,1,0:T(8,128)} async-done(((f32[4,128,128]{2,1,0:T(8,128)}), f32[128,128,128]{2,1,0:T(8,128)}) %all-gather.8.cloned.1.call-update) | async-done | bytes 8388624 | tf_op jit(solution)/shard_map/all_gather | solution.py:108
  230.8 12.3 %fusion.4 = f32[4,1,128,128]{3,1,2,0:T(1,128)S(1)} fusion(f32[32,4,1,1]{0,2,3,1:T(1,128)S(1)} %copy.109, f32[32,4,128,128]{3,2,1,0:T(8,128)} %bitcast.205), kind=kOutput, calls=%fused_computation.10 | convolution fusion | flops 25165824 | bytes 8651264 | tf_op jit(solution)/shard_map/jh,jhde->hde/dot_general | solution.py:105
  244.7 2.5 fusion.48
  247.7 2.1 convolution_multiply_fusion.13
  251.0 2.4 multiply_reduce_fusion.12
  254.1 2.1 convolution_multiply_fusion.11
  257.8 2.4 multiply_reduce_fusion.10
  260.6 2.1 convolution_multiply_fusion.9
  263.9 2.4 multiply_reduce_fusion.8
  266.8 2.1 convolution_multiply_fusion.7
  270.0 2.6 multiply_reduce_fusion.6
  273.0 2.1 convolution_multiply_fusion.5
  276.3 2.4 multiply_reduce_fusion.4
  279.1 2.1 convolution_multiply_fusion.3
  282.4 2.4 multiply_reduce_fusion.2
  285.5 2.3 convolution_multiply_fusion.1
  289.0 2.4 fusion.24
  292.7 2.1 convolution_multiply_fusion
  298.5 7.8 %fusion.70 = f32[512,4096]{1,0:T(8,128)} fusion(bf16[512,4096]{1,0:T(8,128)(2,1)} %param.13, f32[64,8,4,128]{3,2,1,0:T(4,128)S(1)} %bitcast.206, f32[64,8,4,128]{3,2,1,0:T(4,128)S(1)} %bitcast.207), kind=kOutput, calls=%fused_computation.138 | convolution fusion | flops 2148007936 | bytes 14680064 | tf_op jit(solution)/shard_map/dot_general | solution.py:119
  306.3 52.4 %reduce-scatter.2.cloned.1.call-done = f32[64,4096]{1,0:T(8,128)} async-done(((f32[512,4096]{1,0:T(8,128)}), f32[64,4096]{1,0:T(8,128)}) %reduce-scatter.2.cloned.1.call-update) | async-done | bytes 1048592 | tf_op jit(solution)/shard_map/reduce_scatter | solution.py:118
  358.7 2.1 convert_element_type.16
  (117 shorter events, 40.8 us)
Async XLA Ops:
  6.5 8.6 %copy-start.5 = (bf16[512,512]{1,0:T(8,128)(2,1)S(1)}, bf16[512,512]{1,0:T(8,128)(2,1)}, u32[]{:S(2)}) copy-start(bf16[512,512]{1,0:T(8,128)(2,1)} %param.10) | copy-start | bytes 1572868
  6.5 126.7 %all-gather.6.cloned.1.call-start = ((), (), s32[]{:S(2)}) async-start(), calls=%async_computation.2 | async-start | bytes 8650752 | tf_op jit(solution)/shard_map/all_gather | solution.py:102
  21.1 11.8 %copy-start.7 = (u32[256]{0:T(256)S(1)}, u32[256]{0:T(256)}, u32[]{:S(2)}) copy-start(u32[256]{0:T(256)} %constant.48) | copy-start | bytes 3076
  31.4 0.7 copy-start
  31.4 0.8 copy-start.1
  32.1 198.7 %all-gather.8.cloned.1.call-start = ((), (), s32[]{:S(2)}) async-start(), calls=%async_computation.3 | async-start | bytes 8650752 | tf_op jit(solution)/shard_map/all_gather | solution.py:108
  32.9 325.8 %reduce-scatter.2.cloned.1.call-start = ((), (), s32[]{:S(2)}) async-start(), calls=%async_computation.1 | async-start | bytes 9437184 | tf_op jit(solution)/shard_map/reduce_scatter | solution.py:118
  145.3 99.4 %copy-start.6 = (f32[512]{0:T(512)S(1)}, f32[512]{0:T(512)}, u32[]{:S(2)}) copy-start(f32[512]{0:T(512)} %param.12) | copy-start | bytes 6148
  230.8 12.3 %copy-start.3 = (f32[4,4,128,128]{3,2,1,0:T(8,128)S(1)}, f32[4,4,128,128]{3,2,1,0:T(8,128)}, u32[]{:S(2)}) copy-start(f32[4,4,128,128]{3,2,1,0:T(8,128)} %get-tuple-element.65) | copy-start | bytes 3145732
  230.8 12.4 %copy-start.4 = (f32[4,4,128,128]{3,2,1,0:T(8,128)S(1)}, f32[4,4,128,128]{3,2,1,0:T(8,128)}, u32[]{:S(2)}) copy-start(f32[4,4,128,128]{3,2,1,0:T(8,128)} %get-tuple-element.67) | copy-start | bytes 3145732
  230.8 13.9 %copy-start.2 = (f32[4,4,128,128]{3,2,1,0:T(8,128)S(1)}, f32[4,4,128,128]{3,2,1,0:T(8,128)}, u32[]{:S(2)}) copy-start(f32[4,4,128,128]{3,2,1,0:T(8,128)} %convolution_multiply_fusion.15) | copy-start | bytes 3145732
Sparse Core Ops, SparseCore 0:
  32.3 100.9 all-gather.5
  135.9 94.9 all-gather.7
  306.4 52.2 reduce-scatter.1
where the time goes:
time: 373 us; the launch traced here: 368 us
  waiting for transfers between devices  160 us (43%)
  matrix products  89.4 us (24%)
  blocking collectives  65.5 us (18%)
  other arithmetic  22.3 us (6%)
  local copies, waits for them, and re-layouts  15.6 us (4%)
  between operations  14.5 us (4%)
    all_gather x1, waiting for transfers between devices, body(): lax.all_gather(device_g[None], 'seq', axis=0, tiled=True)  85.5 us
    unnamed x1, blocking collectives  65.5 us
    reduce_scatter x1, waiting for transfers between devices, body(): lax.psum_scatter(jnp.dot(normed, out_weight, preferred_element_type=jnp.f...  52.4 us
    all_gather x1, waiting for transfers between devices, body(): lax.all_gather(device_h[None], 'seq', axis=0, tiled=True)  21.4 us
    dot_general x8, matrix products, span_read(): jnp.einsum('...ts,...sd->...td', operate_scores, key_rows, precision=high...  19.5 us
    dot_general x8, matrix products, span_read(): jnp.einsum('...td,...sd->...ts', direction, key_rows, precision=highest)  18.1 us
    dot_general x1, matrix products, body(): jnp.einsum('jh,jhde->hde', weights, lax.all_gather(device_g[None], 'seq',...  12.3 us
    dot_general x1, matrix products, body(): jnp.einsum('jh,jhde->hde', weights, lax.all_gather(device_h[None], 'seq',...  12 us
  transfers between devices with their start and end apart: 3, of which 3 were waited for; matrix products, arithmetic and copies ran while one was open for 7% of the time, Pallas kernels for 0%

commit v1 on v0

--- a/solution.py
+++ b/solution.py
@@ -2,11 +2,19 @@
 import jax.numpy as jnp
 from jax import lax
 from jax.sharding import PartitionSpec as P
+from jax.lax import all_to_all, axis_size
 
 HD = 128
 SPAN = 128
 ITERS = 8
 highest = lax.Precision.HIGHEST
+
+
+def _lay_circles(frame_in, d0):
+    opened = axis_size("seq")
+    current_arr = jnp.stack([frame_in] * opened, 0)
+    w_next = all_to_all(current_arr, axis_name="seq", split_axis=0, concat_axis=0)
+    return jnp.concatenate(w_next, d0)
 
 
 def unit_rows(matrix, head_count, head_size):
@@ -103,10 +111,7 @@
         precision=highest,
     )
     added_g = jnp.einsum(
-        "jh,jhde->hde",
-        weights,
-        lax.all_gather(device_g[None], "seq", axis=0, tiled=True),
-        precision=highest,
+        "jh,jhde->hde", weights, _lay_circles(device_g[None], 0), precision=highest
     )
     lifted = jnp.exp(before_decay)[..., None, None]
     start_h = (lifted * added_h[None] + preceding_memory_h).transpose(1, 0, 2, 3)

time: 373 us -> 509 us (1.36)
  blocking collectives: 65.5 us -> 285 us
  waiting for transfers between devices: 160 us -> 61.6 us
  starting transfers between devices: 0.08 us -> 12.3 us
    unnamed x1, blocking collectives: 65.5 us -> 285 us
    all_gather x1 -> x0, waiting for transfers between devices: 85.5 us -> none  [body(): lax.all_gather(device_g[None], 'seq', axis=0, tiled=True)]
    all_gather x1, waiting for transfers between devices: 21.4 us -> 0.01 us  [body(): lax.all_gather(device_h[None], 'seq', axis=0, tiled=True)]
    all_to_all x0 -> x1, starting transfers between devices: none -> 12.3 us  [_lay_circles(): all_to_all(current_arr, axis_name='seq', split_axis=0, concat_axis=0)]
    reduce_scatter x1, waiting for transfers between devices: 52.4 us -> 61.6 us  [body(): lax.psum_scatter(jnp.dot(normed, out_weight, preferred_element_type=jnp.f...]
  transfers between devices with their start and end apart: 3 -> 3, of which waited for: 3 -> 1; matrix products, arithmetic and copies ran while one was open for 7% -> 5% of each run, Pallas kernels for 0% -> 0%
where the time goes in v1:
time: 509 us; the launch traced here: 503 us
  blocking collectives  285 us (56%)
  matrix products  89.6 us (18%)
  waiting for transfers between devices  61.6 us (12%)
  other arithmetic  21.2 us (4%)
  local copies, waits for them, and re-layouts  18.8 us (4%)
  between operations  14.8 us (3%)
  starting transfers between devices  12.3 us (2%)
    unnamed x1, blocking collectives  285 us
    reduce_scatter x1, waiting for transfers between devices, body(): lax.psum_scatter(jnp.dot(normed, out_weight, preferred_element_type=jnp.f...  61.6 us
    dot_general x8, matrix products, span_read(): jnp.einsum('...ts,...sd->...td', operate_scores, key_rows, precision=high...  19.8 us
    dot_general x8, matrix products, span_read(): jnp.einsum('...td,...sd->...ts', direction, key_rows, precision=highest)  18.1 us
    dot_general x1, matrix products, body(): jnp.einsum('jh,jhde->hde', weights, _lay_circles(device_g[None], 0), prec...  12.4 us
    all_to_all x1, starting transfers between devices, _lay_circles(): all_to_all(current_arr, axis_name='seq', split_axis=0, concat_axis=0)  12.3 us
    dot_general x1, matrix products, body(): jnp.einsum('jh,jhde->hde', weights, lax.all_gather(device_h[None], 'seq',...  12 us
  transfers between devices with their start and end apart: 3, of which 1 were waited for; matrix products, arithmetic and copies ran while one was open for 5% of the time, Pallas kernels for 0%

profile of v1, /device:TPU:1, one launch (start us, length us, event | category | flops | bytes accessed | tf_op | source)
XLA Modules:
  0.0 503.1 jit_solution(8088460955005720548)
XLA Ops:
  12.7 1.9 reduce_sum.173
  15.6 2.3 fusion.10
  17.9 3.2 convolution_bitcast_fusion.1
  23.4 7.9 %while.21 = (s32[]{:T(128)}, f32[4,128,128]{2,1,0:T(8,128)S(1)}, f32[4,128,128]{2,1,0:T(8,128)S(1)}, f32[4]{0:T(128)S(1)}, f32[4,4,128,128]{3,2,1,0:T(8,128)}, /...) while((s32[]{:T(128)}, f32[4,128,128]{2,1,0:T(8,128)S(1)}, ...), condition=%wide.region_5.6_spmd.clone, body=%wide.region_4.5_spmd.clone.sunk | while | flops 524299 | bytes 2622221 | solution.py:92
  32.1 4.3 stack.3
  36.3 12.3 %all-to-all-start = ((f32[32,1,4,128,128]{4,3,2,1,0:T(8,128)}), f32[32,1,4,128,128]{4,3,2,1,0:T(8,128)}, u32[]{:S(2)}, u32[]{:S(2)}) async-start(f32[32,1,4,128,128]{4,3,2,1,0:T(8,128)} %stack.3), calls=%async_computation | async-start | bytes 16777216 | tf_op jit(solution)/shard_map/all_to_all | solution.py:16
  50.2 284.7 %all-reduce = f32[128]{0:T(128)S(1)} all-reduce(f32[128]{0:T(128)S(1)} %dynamic-update-slice), channel_id=2, replica_groups=mesh['seq'=32,'wide'=8] {'seq'}, use_global_device_ids=true, to_apply=%add | all-reduce | flops 128 | bytes 1024
  335.2 1.4 reshape.181
  337.7 1.6 mul.229
  340.1 1.6 copy.60
  341.7 3.1 convolution_multiply_fusion.15
  344.8 12.0 %fusion.6 = f32[4,1,128,128]{3,1,2,0:T(1,128)S(1)} fusion(f32[32,4,1,1]{0,2,3,1:T(1,128)S(1)} %copy.109, f32[32,4,128,128]{3,2,1,0:T(8,128)} %bitcast.204), kind=kOutput, calls=%fused_computation.12 | convolution fusion | flops 25165824 | bytes 8651264 | tf_op jit(solution)/shard_map/jh,jhde->hde/dot_general | solution.py:107
  356.9 12.4 %fusion.4 = f32[4,1,128,128]{3,1,2,0:T(1,128)S(1)} fusion(f32[32,4,1,1]{0,2,3,1:T(1,128)S(1)} %copy.109, f32[32,4,128,128]{3,2,1,0:T(8,128)} %bitcast.18), kind=kOutput, calls=%fused_computation.10 | convolution fusion | flops 25165824 | bytes 8651264 | tf_op jit(solution)/shard_map/jh,jhde->hde/dot_general | solution.py:113
  370.7 2.5 fusion.48
  373.8 2.1 convolution_multiply_fusion.13
  377.1 2.4 multiply_reduce_fusion.12
  380.2 2.1 convolution_multiply_fusion.11
  383.7 2.4 multiply_reduce_fusion.10
  386.5 2.1 convolution_multiply_fusion.9
  389.8 2.4 multiply_reduce_fusion.8
  392.6 2.1 convolution_multiply_fusion.7
  395.9 2.9 multiply_reduce_fusion.6
  399.2 2.1 convolution_multiply_fusion.5
  402.5 2.4 multiply_reduce_fusion.4
  405.3 2.1 convolution_multiply_fusion.3
  408.6 2.4 multiply_reduce_fusion.2
  411.6 2.3 convolution_multiply_fusion.1
  415.1 2.4 fusion.24
  418.9 2.1 convolution_multiply_fusion
  424.6 7.8 %fusion.70 = f32[512,4096]{1,0:T(8,128)} fusion(bf16[512,4096]{1,0:T(8,128)(2,1)} %param.13, f32[64,8,4,128]{3,2,1,0:T(4,128)S(1)} %bitcast.205, f32[64,8,4,128]{3,2,1,0:T(4,128)S(1)} %bitcast.206), kind=kOutput, calls=%fused_computation.138 | convolution fusion | flops 2148007936 | bytes 14680064 | tf_op jit(solution)/shard_map/dot_general | solution.py:124
  432.4 61.6 %reduce-scatter.2.cloned.1.call-done = f32[64,4096]{1,0:T(8,128)} async-done(((f32[512,4096]{1,0:T(8,128)}), f32[64,4096]{1,0:T(8,128)}) %reduce-scatter.2.cloned.1.call-update) | async-done | bytes 1048592 | tf_op jit(solution)/shard_map/reduce_scatter | solution.py:123
  494.0 2.1 convert_element_type.16
  (117 shorter events, 39.3 us)
Async XLA Ops:
  6.5 8.6 %copy-start.5 = (bf16[512,512]{1,0:T(8,128)(2,1)S(1)}, bf16[512,512]{1,0:T(8,128)(2,1)}, u32[]{:S(2)}) copy-start(bf16[512,512]{1,0:T(8,128)(2,1)} %param.10) | copy-start | bytes 1572868
  6.5 338.3 %all-gather.4.cloned.1.call-start = ((), (), s32[]{:S(2)}) async-start(), calls=%async_computation.3 | async-start | bytes 8650752 | tf_op jit(solution)/shard_map/all_gather | solution.py:110
  31.3 0.7 copy-start
  36.3 12.4 %copy-start.7 = (u32[256]{0:T(256)S(1)}, u32[256]{0:T(256)}, u32[]{:S(2)}) copy-start(u32[256]{0:T(256)} %constant.48) | copy-start | bytes 3076
  36.3 298.9 %copy-start.4 = (bf16[512,512]{1,0:T(8,128)(2,1)S(1)}, bf16[512,512]{1,0:T(8,128)(2,1)}, u32[]{:S(2)}) copy-start(bf16[512,512]{1,0:T(8,128)(2,1)} %param.8) | copy-start | bytes 1572868
  36.3 320.5 %all-to-all-start = ((f32[32,1,4,128,128]{4,3,2,1,0:T(8,128)}), f32[32,1,4,128,128]{4,3,2,1,0:T(8,128)}, u32[]{:S(2)}, u32[]{:S(2)}) async-start(f32[32,1,4,128,128]{4,3,2,1,0:T(8,128)} %stack.3), calls=%async_computation | async-start | bytes 16777216 | tf_op jit(solution)/shard_map/all_to_all | solution.py:16
  48.6 445.3 %reduce-scatter.2.cloned.1.call-start = ((), (), s32[]{:S(2)}) async-start(), calls=%async_computation.2 | async-start | bytes 9437184 | tf_op jit(solution)/shard_map/reduce_scatter | solution.py:123
  356.8 13.9 %copy-start.6 = (f32[512]{0:T(512)S(1)}, f32[512]{0:T(512)}, u32[]{:S(2)}) copy-start(f32[512]{0:T(512)} %param.12) | copy-start | bytes 6148
  356.8 12.4 %copy-start.2 = (f32[4,4,128,128]{3,2,1,0:T(8,128)S(1)}, f32[4,4,128,128]{3,2,1,0:T(8,128)}, u32[]{:S(2)}) copy-start(f32[4,4,128,128]{3,2,1,0:T(8,128)} %get-tuple-element.65) | copy-start | bytes 3145732
  356.8 12.4 %copy-start.3 = (f32[4,4,128,128]{3,2,1,0:T(8,128)S(1)}, f32[4,4,128,128]{3,2,1,0:T(8,128)}, u32[]{:S(2)}) copy-start(f32[4,4,128,128]{3,2,1,0:T(8,128)} %get-tuple-element.67) | copy-start | bytes 3145732
  356.9 13.9 %copy-start.1 = (f32[4,4,128,128]{3,2,1,0:T(8,128)S(1)}, f32[4,4,128,128]{3,2,1,0:T(8,128)}, u32[]{:S(2)}) copy-start(f32[4,4,128,128]{3,2,1,0:T(8,128)} %convolution_multiply_fusion.15) | copy-start | bytes 3145732
Sparse Core Ops, SparseCore 0:
  32.2 213.3 all-gather.3
  432.5 61.4 reduce-scatter.1
